TPU v7x, 256 devices: a whole 4x4x8 slice. The times are simulated.
256 devices in a mesh: wide: 32 (over x, z), narrow: 8 (over y, core).
Axes of the slice: x: 4, y: 4, z: 8, core: 2. Of those that a mesh axis runs over, the one named last changes fastest.
Arguments:
- tile_data: bfloat16 [81920, 128, 128], P(('wide', 'narrow')), may hold values from -0.119628906 to 0.119628906
- tile_user: int32 [81920], P(('wide', 'narrow')), may hold values from 0 to 63
- tile_item: int32 [81920], P(('wide', 'narrow')), may hold values from 0 to 31
- tile_word: int32 [81920], P(('wide', 'narrow')), may hold values from 0 to 4095
- tile_month: int32 [81920], P(('wide', 'narrow')), may hold values from 0 to 999
- tile_live: int32 [256], P(('wide', 'narrow')), may hold values from 160 to 320, as said below
- user_need: int32 [256, 64], P(('wide', 'narrow')), may hold values from 0 to 511, as said below
- item_need: int32 [256, 32], P(('wide', 'narrow')), may hold values from 0 to 511, as said below
- user_slot: int32 [512], replicated, may hold values from 0 to 511, as said below
- item_slot: int32 [512], replicated, may hold values from 0 to 511, as said below
- user_factor: bfloat16 [65536, 128], P('wide'), may hold values from -6 to 6
- word_factor: bfloat16 [4096, 128], replicated, may hold values from -6 to 6
- month_factor: bfloat16 [1000, 128], replicated, may hold values from -6 to 6
Outputs:
- item_rows: float32 [65536, 128], P(('wide', 'narrow'))
Inputs may be any that keep to these rules, and one draw needn't show every extreme that they name: user_slot is a permutation; the owner of user block b is user_slot[b] // 16. item_slot is a permutation; the owner of item block b is item_slot[b] // 16. `user_need`: entries k * 2 to k * 2 + 1 of each row are distinct user blocks whose owner is k. `item_need`: entry k of each row is an item block whose owner is k. `tile_live`: some device has all its slots live.
All inputs are finite; a program needn't handle non-finite values.
Results may differ from a plain program's by a relative error of at most 0.0029.
Values may be sent and summed in bfloat16 or wider, within the bound.
A program may use at most 128 MiB of HBM per device.

v0:
```python
import jax
import jax.numpy as jnp
from jax import lax
from jax.sharding import PartitionSpec as P


def shards(
    tile_data,
    tile_user,
    tile_item,
    tile_word,
    tile_month,
    tile_live,
    user_need,
    item_need,
    user_slot,
    item_slot,
    user_factor,
    word_factor,
    month_factor,
):
    wide_count = lax.axis_size("wide")
    tile_count = tile_data.shape[0]
    block_side = tile_data.shape[1]
    rank_width = user_factor.shape[1]
    items_owned = item_slot.shape[0] // wide_count
    touched = item_need.shape[1]
    item_local = (item_slot[item_need[0]] % items_owned).reshape(wide_count, -1)
    item_from = lax.all_to_all(item_local, "wide", split_axis=0, concat_axis=0, tiled=True)
    user_place = user_slot[user_need[0]]
    gathered = lax.all_gather(user_factor, "wide", axis=0, tiled=True)
    fetched = gathered.reshape(-1, block_side, rank_width)[user_place]
    word_month = word_factor[tile_word].astype(jnp.float32) * month_factor[tile_month].astype(
        jnp.float32
    )
    scaled = (fetched[tile_user].astype(jnp.float32) * word_month[:, None, :]).astype(jnp.bfloat16)
    contrib = jnp.einsum("tab,tar->tbr", tile_data, scaled, preferred_element_type=jnp.float32)
    is_live = lax.iota(jnp.int32, tile_count) < tile_live[0]
    group_ids = jnp.where(is_live, tile_item, touched)
    partial_value = jax.ops.segment_sum(contrib, group_ids, num_segments=touched + 1)[:touched]
    arrived = lax.all_to_all(
        partial_value.reshape(wide_count, -1, block_side, rank_width),
        "wide",
        split_axis=0,
        concat_axis=0,
        tiled=True,
    )
    arrived = arrived.reshape(-1, block_side, rank_width)
    slot_ids = item_from.reshape(-1)
    placing = (slot_ids[:, None] == lax.iota(jnp.int32, items_owned)[None, :]).astype(jnp.float32)
    owner_sum = jnp.einsum("kj,kbr->jbr", placing, arrived, precision=lax.Precision.HIGHEST)
    owned_rows = lax.psum_scatter(owner_sum, "narrow", scatter_dimension=0, tiled=True)
    return owned_rows.reshape(-1, rank_width)


def solution(mesh):
    return jax.shard_map(
        shards,
        mesh=mesh,
        in_specs=(
            P(("wide", "narrow"), None, None),
            P(("wide", "narrow")),
            P(("wide", "narrow")),
            P(("wide", "narrow")),
            P(("wide", "narrow")),
            P(("wide", "narrow")),
            P(("wide", "narrow"), None),
            P(("wide", "narrow"), None),
            P(),
            P(),
            P("wide", None),
            P(),
            P(),
        ),
        out_specs=P(("wide", "narrow"), None),
        check_vma=False,
    )
```

profile of v0, /device:TPU:1, one launch (start us, length us, event | category | flops | bytes accessed | tf_op | source)
XLA Modules:
  0.0 344.7 jit_solution(6248891772234273754)
XLA Ops:
  6.5 0.0 copy-start
  6.5 0.0 all-gather.2.cloned.1.call-start
  6.5 0.7 all-gather.2.cloned.1.call-update
  7.3 0.7 fusion.11
  7.9 1.4 gather_fusion
  9.3 0.7 copy.26
  10.0 11.9 %all-to-all-start = ((s32[32,1,1]{2,1,0:T(1,128)}), s32[32,1,1]{2,1,0:T(1,128)S(1)}, u32[]{:S(2)}, u32[]{:S(2)}) async-start(s32[32,1,1]{2,1,0:T(1,128)} %copy.26), calls=%async_computation | async-start | bytes 32768 | tf_op jit(solution)/shard_map/all_to_all | solution.py:29
  22.5 0.7 fusion.12
  23.2 1.5 gather_fusion.1
  24.7 0.7 compare_select_fusion.1
  25.4 0.0 copy-done
  25.4 1.4 gather_fusion.4
  26.8 0.7 compare_select_fusion
  27.5 2.1 gather_fusion.5
  29.7 0.7 compare_select_fusion.2
  30.4 0.7 fusion.9
  31.1 122.8 %all-gather.2.cloned.1.call-done = bf16[65536,128]{1,0:T(8,128)(2,1)} async-done(((bf16[2048,128]{1,0:T(8,128)(2,1)}), bf16[65536,128]{1,0:T(8,128)(2,1)}) %all-gather.2.cloned.1.call-update) | async-done | bytes 16777232 | tf_op jit(solution)/shard_map/all_gather | solution.py:31
  153.9 6.7 %gather_fusion.2 = bf16[64,128,128]{2,1,0:T(8,128)(2,1)S(1)} fusion(bf16[512,128,128]{2,1,0:T(8,128)(2,1)} %bitcast.31, s32[1024]{0:T(1024)S(1)} %pad_clamp_fusion.3), kind=kCustom, calls=%fused_computation.2 | custom fusion | bytes 4194560 | tf_op jit(solution)/shard_map/gather | solution.py:32
  160.6 10.7 %gather_fusion.3 = bf16[320,128,128]{2,1,0:T(8,128)(2,1)} fusion(bf16[64,128,128]{2,1,0:T(8,128)(2,1)S(1)} %gather_fusion.2, s32[1024]{0:T(1024)S(1)} %pad_clamp_fusion.2), kind=kCustom, calls=%fused_computation.3 | custom fusion | bytes 20972800 | tf_op jit(solution)/shard_map/gather | solution.py:36
  171.4 12.9 %fusion.2 = f32[320,128,128]{1,2,0:T(8,128)} fusion(bf16[320,128,128]{2,1,0:T(8,128)(2,1)} %param.13, bf16[320,128,128]{2,1,0:T(8,128)(2,1)} %gather_fusion.3, f32[320,128]{1,0:T(8,128)S(1)} %convert_multiply_fusion), kind=kOutput, calls=%fused_computation.10 | convolution fusion | flops 1357905920 | bytes 42106880 | tf_op jit(solution)/shard_map/tab,tar->tbr/dot_general | solution.py:37
  184.3 21.1 %copy.28 = f32[320,128,128]{2,1,0:T(8,128)} copy(f32[320,128,128]{1,2,0:T(8,128)} %fusion.2) | data formatting | bytes 41943040 | tf_op jit(solution)/shard_map/tab,tar->tbr/dot_general | solution.py:37
  205.4 0.2 broadcast_in_dim.24
  205.7 0.0 copy-start.1
  205.7 41.9 %scatter_fusion = f32[33,128,128]{2,1,0:T(8,128)S(1)} fusion(f32[33,128,128]{2,1,0:T(8,128)S(1)} %broadcast_in_dim.24, s32[320]{0:T(512)S(1)} %fusion.9, f32[320,128,128]{2,1,0:T(8,128)} %copy.28), kind=kCustom, calls=%fused_computation.6 | custom fusion | flops 5242880 | bytes 62915840 | tf_op jit(solution)/shard_map/scatter-add | solution.py:40
  247.6 1.5 slice_bitcast_fusion
  249.1 0.0 all-to-all-done
  249.1 5.3 %all-to-all-start.1 = ((f32[32,1,128,128]{3,2,1,0:T(8,128)}), f32[32,1,128,128]{3,2,1,0:T(8,128)S(1)}, u32[]{:S(2)}, u32[]{:S(2)}) async-start(f32[32,1,128,128]{3,2,1,0:T(8,128)} %slice_bitcast_fusion), calls=%async_computation.1 | async-start | bytes 4194304 | tf_op jit(solution)/shard_map/all_to_all | solution.py:41
  254.4 0.0 reduce-scatter.2.cloned.1.call-start
  254.4 0.7 reduce
  255.1 48.0 %all-to-all-done.1 = f32[32,1,128,128]{3,2,1,0:T(8,128)S(1)} async-done(((f32[32,1,128,128]{3,2,1,0:T(8,128)}), f32[32,1,128,128]{3,2,1,0:T(8,128)S(1)}, u32[]{:S(2)}, u32[]{:S(2)}) %all-to-all-start.1) | async-done | bytes 2097184 | tf_op jit(solution)/shard_map/all_to_all | solution.py:41
  303.1 2.0 fusion.3
  305.1 1.3 copy.31
  306.4 0.0 reduce-scatter.2.cloned.1.call-update
  306.4 31.5 %reduce-scatter.2.cloned.1.call-done = f32[2,128,128]{2,1,0:T(8,128)} async-done(((f32[16,128,128]{2,1,0:T(8,128)}), f32[2,128,128]{2,1,0:T(8,128)}) %reduce-scatter.2.cloned.1.call-update) | async-done | bytes 131088 | tf_op jit(solution)/shard_map/reduce_scatter | solution.py:52
  337.9 0.0 copy-done.1
  (9 shorter events, 0.1 us)
Async XLA Ops:
  6.5 18.9 %copy-start = (bf16[4096,128]{1,0:T(8,128)(2,1)S(1)}, bf16[4096,128]{1,0:T(8,128)(2,1)}, u32[]{:S(2)}) copy-start(bf16[4096,128]{1,0:T(8,128)(2,1)} %param.24) | copy-start | bytes 3145732
  6.5 147.4 %all-gather.2.cloned.1.call-start = ((), (), s32[]{:S(2)}) async-start(), calls=%async_computation.3 | async-start | bytes 17301504 | tf_op jit(solution)/shard_map/all_gather | solution.py:31
  10.0 239.1 %all-to-all-start = ((s32[32,1,1]{2,1,0:T(1,128)}), s32[32,1,1]{2,1,0:T(1,128)S(1)}, u32[]{:S(2)}, u32[]{:S(2)}) async-start(s32[32,1,1]{2,1,0:T(1,128)} %copy.26), calls=%async_computation | async-start | bytes 32768 | tf_op jit(solution)/shard_map/all_to_all | solution.py:29
  205.7 132.2 %copy-start.1 = (bf16[4096,128]{1,0:T(8,128)(2,1)S(1)}, bf16[4096,128]{1,0:T(8,128)(2,1)}, u32[]{:S(2)}) copy-start(bf16[4096,128]{1,0:T(8,128)(2,1)} %param.24) | copy-start | bytes 3145732
  249.1 53.9 %all-to-all-start.1 = ((f32[32,1,128,128]{3,2,1,0:T(8,128)}), f32[32,1,128,128]{3,2,1,0:T(8,128)S(1)}, u32[]{:S(2)}, u32[]{:S(2)}) async-start(f32[32,1,128,128]{3,2,1,0:T(8,128)} %slice_bitcast_fusion), calls=%async_computation.1 | async-start | bytes 4194304 | tf_op jit(solution)/shard_map/all_to_all | solution.py:41
  254.4 83.5 %reduce-scatter.2.cloned.1.call-start = ((), (), s32[]{:S(2)}) async-start(), calls=%async_computation.4 | async-start | bytes 1179648 | tf_op jit(solution)/shard_map/reduce_scatter | solution.py:52
Sparse Core Ops, SparseCore 0:
  10.0 143.9 all-gather.1
  306.5 31.3 reduce-scatter.1
where the time goes:
time: 348 us; the launch traced here: 345 us
  waiting for transfers between devices  203 us (58%)
  local copies, waits for them, and re-layouts  48.7 us (14%)
  other arithmetic  46.7 us (13%)
  starting transfers between devices  17.2 us (5%)
  matrix products  14.9 us (4%)
  between operations  14.1 us (4%)
    all_gather x1, waiting for transfers between devices, shards(): gathered = lax.all_gather(user_factor, 'wide', axis=0, tiled=True)  123 us
    all_to_all x1, waiting for transfers between devices, shards(): lax.all_to_all(partial_value.reshape(wide_count, -1, block_side, rank_wid...  48 us
    scatter-add x1, other arithmetic, shards(): jax.ops.segment_sum(contrib, group_ids, num_segments=touched + 1)[:touched]  41.9 us
    reduce_scatter x1, waiting for transfers between devices, shards(): lax.psum_scatter(owner_sum, 'narrow', scatter_dimension=0, tiled=True)  31.5 us
    dot_general x1, local copies, waits for them, and re-layouts, shards(): jnp.einsum('tab,tar->tbr', tile_data, scaled, preferred_element_type=jnp....  21.1 us
    dot_general x1, matrix products, shards(): jnp.einsum('tab,tar->tbr', tile_data, scaled, preferred_element_type=jnp....  12.9 us
    all_to_all x1, starting transfers between devices, shards(): lax.all_to_all(item_local, 'wide', split_axis=0, concat_axis=0, tiled=True)  11.9 us
    gather x1, local copies, waits for them, and re-layouts, shards(): fetched[tile_user].astype(jnp.float32) * word_month[:, None, :]  10.7 us
  transfers between devices with their start and end apart: 4, of which 3 were waited for; matrix products, arithmetic and copies ran while one was open for 31% of the time, Pallas kernels for 0%

commit v1 on v0

v1 whole, which is shorter than its diff:
```python
import functools

import jax
import jax.numpy as jnp
from jax import lax
from jax.experimental import pallas as pl
from jax.experimental.pallas import tpu as pltpu
from jax.sharding import PartitionSpec as P

MESH = pl.DeviceIdType.MESH
ANY = pl.BlockSpec(memory_space=pl.ANY)
VMEM = pl.BlockSpec(memory_space=pltpu.VMEM)
SMEM = pl.BlockSpec(memory_space=pltpu.SMEM)
DMA = pltpu.SemaphoreType.DMA


def place(zs):
    wide, n = lax.axis_index("wide"), lax.axis_index("narrow")
    return wide // zs, lax.rem(wide, zs), n


def fetch_kernel(
    peers, ns, upo, needs, factor, fetched, table, held, packed, landed, table_s,
    local_sem, table_send, table_recv, line_send, line_recv, pack_send, pack_recv,
):
    zs = qs = ns
    x, z, n = place(zs)
    me = x * ns + n

    def plane(p):
        return (p // ns * zs + z, lax.rem(p, ns))

    def line(d):
        return (x * zs + lax.rem(z + d, zs), n)

    barrier = pltpu.get_barrier_semaphore()

    @pl.loop(1, peers)
    def _(r):
        pl.semaphore_signal(barrier, inc=1, device_id=plane(lax.rem(me + r, peers)), device_id_type=MESH)

    @pl.loop(1, zs)
    def _(d):
        pl.semaphore_signal(barrier, inc=1, device_id=line(d), device_id_type=MESH)

    pl.semaphore_wait(barrier, peers - 1 + zs - 1)

    def table_copy(p, slot, r):
        return pltpu.make_async_remote_copy(
            src_ref=needs, dst_ref=table.at[slot], send_sem=table_send.at[r], recv_sem=table_recv.at[slot],
            device_id=plane(p), device_id_type=MESH,
        )

    def line_copy(d, chunk):
        return pltpu.make_async_remote_copy(
            src_ref=factor.at[:, chunk], dst_ref=held.at[d], send_sem=line_send.at[d], recv_sem=line_recv.at[d],
            device_id=line(zs - d), device_id_type=MESH,
        )

    def pack_copy(p, slot, r):
        return pltpu.make_async_remote_copy(
            src_ref=packed.at[r], dst_ref=landed.at[slot], send_sem=pack_send.at[r], recv_sem=pack_recv.at[slot],
            device_id=plane(p), device_id_type=MESH,
        )

    @pl.loop(1, peers)
    def _(r):
        table_copy(lax.rem(me + r, peers), me, r).start()

    own = pltpu.make_async_copy(factor.at[:, lax.rem(ns - n, qs)], held.at[0], local_sem)
    own.start()

    @pl.loop(1, zs)
    def _(d):
        line_copy(d, lax.rem(d + ns - n, qs)).start()

    table[me] = needs[...]

    @pl.loop(1, peers)
    def _(r):
        p = lax.rem(me + r, peers)
        table_copy(p, p, r).wait_recv()

    own.wait()
    to_scalar = pltpu.make_async_copy(table, table_s, local_sem)
    to_scalar.start()
    to_scalar.wait()

    @pl.loop(1, zs)
    def _(d):
        line_copy(d, 0).wait_recv()

    def pack(p, target, at):
        for d in range(zs):
            owner = x * zs + lax.rem(z + d, zs)
            for i in range(upo):
                target[at, d * upo + i] = held[d, table_s[p, 0, owner * upo + i]]

    @pl.loop(1, peers)
    def _(r):
        p = lax.rem(me + r, peers)
        pack(p, packed, r)
        pack_copy(p, me, r).start()

    pack(me, landed, me)

    def unpack(p):
        px, pn = p // ns, lax.rem(p, ns)
        for d in range(zs):
            owner = px * zs + lax.rem(z + d, zs)
            q = lax.rem(d + ns - pn, qs)
            for i in range(upo):
                fetched[owner * upo + i, q] = landed[p, d * upo + i]

    unpack(me)

    @pl.loop(1, peers)
    def _(r):
        p = lax.rem(me + peers - r, peers)
        pack_copy(p, p, r).wait_recv()
        unpack(p)

    @pl.loop(1, peers)
    def _(r):
        table_copy(me, me, r).wait_send()
        pack_copy(me, me, r).wait_send()

    @pl.loop(1, zs)
    def _(d):
        line_copy(d, 0).wait_send()


def tile_kernel(
    ns, unroll, parts, tile_user, tile_item, live, place_s, data, fetched, scale, packed,
    buffer, total, data_sem,
):
    tiles, touched = buffer.shape[0], total.shape[0] - 1
    zs = qs = ns
    z = place_s[0]
    per = tiles // parts
    rows = packed.shape[2]

    def data_copy(c):
        span = pl.ds(c * per, per)
        return pltpu.make_async_copy(data.at[span], buffer.at[span], data_sem.at[c])

    for c in range(parts):
        data_copy(c).start()
    total[...] = jnp.zeros_like(total)

    def step(s, carry):
        terms = []
        for k in range(unroll):
            t = s * unroll + k
            block = fetched[tile_user[t]].astype(jnp.float32)
            scaled = (block * scale[pl.ds(t, 1), :]).astype(jnp.bfloat16)
            term = lax.dot_general(
                buffer[t], scaled, (((0,), (0,)), ((), ())), preferred_element_type=jnp.float32
            )
            terms.append((jnp.where(t < live[0], tile_item[t], touched), term))
        for item, term in terms:
            total[item] += term
        return carry

    for c in range(parts):
        data_copy(c).wait()
        lax.fori_loop(c * per // unroll, (c + 1) * per // unroll, step, 0)

    @pl.loop(0, touched)
    def _(k):
        kx, d = k // zs, lax.rem(lax.rem(k, zs) + zs - z, zs)
        for q in range(qs):
            pn = lax.rem(d + ns - q, ns)
            packed[kx * ns + pn, q] = total[k, q * rows : (q + 1) * rows, :].astype(packed.dtype)


def reduce_kernel(
    peers, ns, owned, previous, final, packed, out, arrived, sums, leaving, landed,
    local_sem, plane_send, plane_recv, last_send, last_recv,
):
    zs = qs = ns
    x, z, n = place(zs)
    me = x * ns + n
    each = owned // ns

    def plane(p):
        return (p // ns * zs + z, lax.rem(p, ns))

    def sheet(d, m):
        return (x * zs + lax.rem(z + d, zs), lax.rem(n + m, ns))

    barrier = pltpu.get_barrier_semaphore()

    @pl.loop(1, peers)
    def _(r):
        pl.semaphore_signal(barrier, inc=1, device_id=plane(lax.rem(me + r, peers)), device_id_type=MESH)

    @pl.loop(1, zs * ns)
    def _(r):
        pl.semaphore_signal(barrier, inc=1, device_id=sheet(r // ns, lax.rem(r, ns)), device_id_type=MESH)

    pl.semaphore_wait(barrier, peers - 1 + zs * ns - 1)

    def plane_copy(p, slot, r):
        return pltpu.make_async_remote_copy(
            src_ref=packed.at[p], dst_ref=arrived.at[slot], send_sem=plane_send.at[r], recv_sem=plane_recv.at[slot],
            device_id=plane(p), device_id_type=MESH,
        )

    @pl.loop(1, peers)
    def _(r):
        plane_copy(lax.rem(me + r, peers), me, r).start()

    own = pltpu.make_async_copy(packed.at[me], arrived.at[me], local_sem)
    own.start()
    sums[0] = jnp.zeros_like(sums[0])
    own.wait()

    @pl.loop(1, peers)
    def _(r):
        p = lax.rem(me + peers - r, peers)
        plane_copy(p, p, r).wait_recv()

    @pl.loop(0, peers)
    def _(i):
        for q in range(qs):
            sums[i + 1, q] = sums[previous[i * qs + q], q] + arrived[i, q].astype(jnp.float32)

    def last_copy(d, m, source, q):
        return pltpu.make_async_remote_copy(
            src_ref=leaving.at[d, lax.rem(n + m, ns)],
            dst_ref=landed.at[source, q],
            send_sem=last_send.at[d * ns + m],
            recv_sem=last_recv.at[source * qs + q],
            device_id=sheet(d, m),
            device_id_type=MESH,
        )

    def leave(d):
        q = lax.rem(d + ns - n, qs)
        for j in range(owned):
            leaving[d, j // each, j % each] = sums[final[q * owned + j], q].astype(leaving.dtype)
        return q

    @pl.loop(1, zs)
    def _(d):
        q = leave(d)

        @pl.loop(0, ns)
        def _(m):
            last_copy(d, m, z, q).start()

    q0 = leave(0)

    @pl.loop(1, ns)
    def _(m):
        last_copy(0, m, z, q0).start()

    landed[z, q0] = leaving[0, n]

    @pl.loop(0, qs)
    def _(q):
        @pl.when(q != q0)
        def _():
            last_copy(1, 0, z, q).wait_recv()

    @pl.loop(1, zs)
    def _(d):
        @pl.loop(0, qs)
        def _(q):
            last_copy(1, 0, lax.rem(z + d, zs), q).wait_recv()

    @pl.loop(0, qs)
    def _(q):
        for s in range(each):
            value = landed[0, q, s].astype(jnp.float32)
            for source in range(1, zs):
                value += landed[source, q, s].astype(jnp.float32)
            out[s, q] = value

    @pl.loop(1, peers)
    def _(r):
        plane_copy(me, me, r).wait_send()

    @pl.loop(1, zs * ns)
    def _(r):
        last_copy(r // ns, lax.rem(r, ns), z, 0).wait_send()


def shards(
    tile_data,
    tile_user,
    tile_item,
    tile_word,
    tile_month,
    tile_live,
    user_need,
    item_need,
    user_slot,
    item_slot,
    user_factor,
    word_factor,
    month_factor,
):
    wide, ns = lax.axis_size("wide"), lax.axis_size("narrow")
    zs = qs = ns
    peers = wide // zs * ns
    tiles, side = tile_data.shape[:2]
    rank = user_factor.shape[1]
    rows = side // qs
    owned_u, owned_i = user_slot.shape[0] // wide, item_slot.shape[0] // wide
    used, touched = user_need.shape[1], item_need.shape[1]
    upo = used // wide
    lanes = -(-(used + touched) // 128) * 128
    x, z, n = place(zs)

    names = jnp.concatenate([user_need[0], item_need[0] + user_slot.shape[0]])
    slots = jnp.concatenate([user_slot % owned_u, item_slot % owned_i])
    hit = names[:, None] == lax.iota(jnp.int32, slots.shape[0])[None, :]
    needs = jnp.sum(jnp.where(hit, slots[None, :], 0), axis=1)
    needs = jnp.pad(needs, (0, lanes - used - touched)).reshape(1, lanes)

    fetched, table = pl.pallas_call(
        functools.partial(fetch_kernel, peers, ns, upo),
        out_shape=(
            jax.ShapeDtypeStruct((used, qs, rows, rank), jnp.bfloat16),
            jax.ShapeDtypeStruct((peers, 1, lanes), jnp.int32),
        ),
        in_specs=[VMEM, ANY],
        out_specs=(VMEM, VMEM),
        scratch_shapes=[
            pltpu.VMEM((zs, owned_u, rows, rank), jnp.bfloat16),
            pltpu.VMEM((peers, zs * upo, rows, rank), jnp.bfloat16),
            pltpu.VMEM((peers, zs * upo, rows, rank), jnp.bfloat16),
            pltpu.SMEM((peers, 1, lanes), jnp.int32),
            DMA,
            DMA((peers,)),
            DMA((peers,)),
            DMA((zs,)),
            DMA((zs,)),
            DMA((peers,)),
            DMA((peers,)),
        ],
        compiler_params=pltpu.CompilerParams(
            collective_id=0, has_side_effects=True, vmem_limit_bytes=20 << 20
        ),
        name="fetch",
    )(needs, user_factor.reshape(owned_u, qs, rows, rank))

    word_month = word_factor[tile_word].astype(jnp.float32) * month_factor[tile_month].astype(jnp.float32)

    packed = pl.pallas_call(
        functools.partial(tile_kernel, ns, 16, tiles // 32 * 2),
        out_shape=jax.ShapeDtypeStruct((peers, qs, rows, rank), jnp.bfloat16),
        grid_spec=pltpu.PrefetchScalarGridSpec(
            num_scalar_prefetch=4,
            grid=(),
            in_specs=[ANY, VMEM, VMEM],
            out_specs=VMEM,
            scratch_shapes=[
                pltpu.VMEM((tiles, side, side), jnp.bfloat16),
                pltpu.VMEM((touched + 1, side, rank), jnp.float32),
                DMA((tiles // 32 * 2,)),
            ],
        ),
        compiler_params=pltpu.CompilerParams(vmem_limit_bytes=40 << 20),
        name="tiles",
    )(
        tile_user, tile_item, tile_live, z.reshape(1),
        tile_data, fetched.reshape(used, side, rank), word_month,
    )

    columns = used + x * zs + (z + (n + lax.iota(jnp.int32, qs)) % zs) % zs
    pick = columns[None, :, None] == lax.iota(jnp.int32, lanes)[None, None, :]
    targets = jnp.sum(jnp.where(pick, table, 0), axis=2)
    order = lax.iota(jnp.int32, peers)
    same = (targets[:, None, :] == targets[None, :, :]) & (order[None, :, None] < order[:, None, None])
    previous = jnp.max(jnp.where(same, order[None, :, None] + 1, 0), axis=1)
    mine = targets[:, :, None] == lax.iota(jnp.int32, owned_i)[None, None, :]
    final = jnp.max(jnp.where(mine, order[:, None, None] + 1, 0), axis=0)

    each = owned_i // ns
    out = pl.pallas_call(
        functools.partial(reduce_kernel, peers, ns, owned_i),
        out_shape=jax.ShapeDtypeStruct((each, qs, rows, rank), jnp.float32),
        in_specs=[SMEM, SMEM, ANY],
        out_specs=VMEM,
        scratch_shapes=[
            pltpu.VMEM((peers, qs, rows, rank), jnp.bfloat16),
            pltpu.VMEM((peers + 1, qs, rows, rank), jnp.float32),
            pltpu.VMEM((zs, ns, each, rows, rank), jnp.bfloat16),
            pltpu.VMEM((zs, qs, each, rows, rank), jnp.bfloat16),
            DMA,
            DMA((peers,)),
            DMA((peers,)),
            DMA((zs * ns,)),
            DMA((zs * qs,)),
        ],
        compiler_params=pltpu.CompilerParams(
            collective_id=1, has_side_effects=True, vmem_limit_bytes=20 << 20
        ),
        name="reduce",
    )(previous.reshape(-1), final.reshape(-1), packed)
    return out.reshape(-1, rank)


def solution(mesh):
    return jax.shard_map(
        shards,
        mesh=mesh,
        in_specs=(
            P(("wide", "narrow"), None, None),
            P(("wide", "narrow")),
            P(("wide", "narrow")),
            P(("wide", "narrow")),
            P(("wide", "narrow")),
            P(("wide", "narrow")),
            P(("wide", "narrow"), None),
            P(("wide", "narrow"), None),
            P(),
            P(),
            P("wide", None),
            P(),
            P(),
        ),
        out_specs=P(("wide", "narrow"), None),
        check_vma=False,
    )
```

time: 348 us -> 135 us (0.39)
  waiting for transfers between devices: 203 us -> 0 us
  Pallas kernels: 0 us -> 118 us
  other arithmetic: 46.7 us -> 5.4 us
  local copies, waits for them, and re-layouts: 48.7 us -> 10.8 us
  starting transfers between devices: 17.2 us -> 0 us
  matrix products: 14.9 us -> 0 us
  between operations: 14.1 us -> 0.75 us
    all_gather x1 -> x0, waiting for transfers between devices: 123 us -> none  [shards(): gathered = lax.all_gather(user_factor, 'wide', axis=0, tiled=True)]
    pallas_call x0 -> x3, Pallas kernels: none -> 118 us  [the longest x1 57.4 us: shards(): pl.pallas_call(functools.partial(fetch_kernel, peers, ns, upo), out_shape...]
    all_to_all x2 -> x0, waiting for transfers between devices: 48 us -> none  [the longest x1 48 us: shards(): lax.all_to_all(partial_value.reshape(wide_count, -1, block_side, rank_wid...]
    scatter-add x1 -> x0, other arithmetic: 41.9 us -> none  [shards(): jax.ops.segment_sum(contrib, group_ids, num_segments=touched + 1)[:touched]]
    reduce_scatter x1 -> x0, waiting for transfers between devices: 31.5 us -> none  [shards(): lax.psum_scatter(owner_sum, 'narrow', scatter_dimension=0, tiled=True)]
    dot_general x2 -> x0, local copies, waits for them, and re-layouts: 22.4 us -> none  [the longest x1 21.1 us: shards(): jnp.einsum('tab,tar->tbr', tile_data, scaled, preferred_element_type=jnp....]
    gather x4 -> x0, local copies, waits for them, and re-layouts: 20.3 us -> none  [the longest x1 10.7 us: shards(): fetched[tile_user].astype(jnp.float32) * word_month[:, None, :]]
    all_to_all x2 -> x0, starting transfers between devices: 17.1 us -> none  [the longest x1 11.9 us: shards(): lax.all_to_all(item_local, 'wide', split_axis=0, concat_axis=0, tiled=True)]
  transfers between devices with their start and end apart: 4 -> 0, of which waited for: 3 -> 0; matrix products, arithmetic and copies ran while one was open for 31% -> 0% of each run, Pallas kernels for 0% -> 0%
where the time goes in v1:
time: 135 us
  Pallas kernels  118 us (87%)
  local copies, waits for them, and re-layouts  10.8 us (8%)
  other arithmetic  5.4 us (4%)
    pallas_call x1, Pallas kernels, shards(): pl.pallas_call(functools.partial(fetch_kernel, peers, ns, upo), out_shape...  57.4 us
    pallas_call x1, Pallas kernels, shards(): pl.pallas_call(functools.partial(reduce_kernel, peers, ns, owned_i), out_...  51.2 us
    pallas_call x1, Pallas kernels, shards(): pl.pallas_call(functools.partial(tile_kernel, ns, 16, tiles // 32 * 2), o...  9.54 us
    unnamed x11, local copies, waits for them, and re-layouts  7.04 us

profile of v1, /device:TPU:1, one launch (start us, length us, event | category | flops | bytes accessed | tf_op | source)
XLA Modules:
  0.0 135.1 jit_solution(1146907418587914627)
XLA Ops:
  0.0 0.0 copy-start
  0.0 0.1 iota_compare_fusion.3
  0.1 0.8 add_select_fusion
  0.9 0.7 add_bitcast_fusion
  1.5 0.7 pad_add_fusion.1
  2.3 0.2 select_reduce_fusion
  2.5 0.0 copy-start.2
  2.5 1.0 copy-done.2
  3.5 57.4 %fetch.1 = (bf16[64,8,16,128]{3,2,1,0:T(8,128)(2,1)S(1)}, s32[32,1,128]{2,1,0:T(1,128)S(1)}) custom-call(s32[1,128]{1,0:T(1,128)S(1)} %pad_bitcast_fusion.needs, bf16[16,8,16,128]{3,2,1,0:T(8,128)(2,1)S(1)} %bitcast.12), custom_call_target="tpu_custom_call" | custom-call | tf_op jit(solution)/shard_map/fetch/pallas_call | solution.py:323
  60.9 0.6 select_reduce_fusion.2
  61.6 0.1 copy.14
  61.6 0.7 select_reduce_fusion.1
  62.3 0.1 reshape.106.previous
  62.4 0.2 select_reduce_fusion.3
  62.6 0.1 reshape.107.final
  62.7 0.7 compare_select_fusion.1
  63.4 0.0 copy-done
  63.4 1.4 %gather_fusion = bf16[320,128]{1,0:T(8,128)(2,1)S(1)} fusion(bf16[4096,128]{1,0:T(8,128)(2,1)S(1)} %copy-done, s32[1024]{0:T(1024)S(1)} %pad_clamp_fusion.1), kind=kCustom, calls=%fused_computation | custom fusion | bytes 165120 | tf_op jit(solution)/shard_map/gather | solution.py:350
  64.8 0.7 compare_select_fusion
  65.5 2.1 %gather_fusion.1 = bf16[320,128]{1,0:T(8,128)(2,1)S(1)} fusion(bf16[1000,128]{1,0:T(8,128)(2,1)} %param.25, s32[1024]{0:T(1024)S(1)} %pad_clamp_fusion), kind=kCustom, calls=%fused_computation.1 | custom fusion | bytes 165120 | tf_op jit(solution)/shard_map/gather | solution.py:350
  68.3 0.0 copy-start.1
  68.3 4.0 %copy-done.1 = bf16[320,128,128]{2,1,0:T(8,128)(2,1)S(1)} copy-done((bf16[320,128,128]{2,1,0:T(8,128)(2,1)S(1)}, bf16[320,128,128]{2,1,0:T(8,128)(2,1)}, u32[]{:S(2)}) %copy-start.1) | copy-done | bytes 10485784
  72.3 0.0 copy-start.3
  72.3 0.7 copy-done.3
  73.0 0.0 copy-start.4
  73.0 0.7 copy-done.4
  73.7 9.5 %tiles.1.packed = bf16[32,8,16,128]{3,2,1,0:T(8,128)(2,1)S(1)} custom-call(s32[320]{0:T(512)S(1)} %copy-done.3, s32[320]{0:T(512)S(1)} %copy-done.4, s32[1]{0:T(128)S(6)} %copy.17.live, s32[1]{0:T(128)} %bitcast.5.place_s, bf16[320,128,128]{2,1,0:T(8,128)(2,1)S(1)} %copy-done.1, bf16[64,128,128]{2,1,0:T(8,128)(2,1)S(1)} %bitcast.10, ...), custom_call_target="tpu_custom_call" | custom-call | tf_op jit(solution)/shard_map/tiles/pallas_call | solution.py:352
  83.2 51.2 %reduce.1 = f32[2,8,16,128]{3,2,1,0:T(8,128)S(1)} custom-call(s32[256]{0:T(256)S(1)} %reshape.106.previous, s32[128]{0:T(128)S(1)} %reshape.107.final, bf16[32,8,16,128]{3,2,1,0:T(8,128)(2,1)S(1)} %tiles.1.packed), custom_call_target="tpu_custom_call" | custom-call | tf_op jit(solution)/shard_map/reduce/pallas_call | solution.py:383
  134.5 0.7 copy.18
  (8 shorter events, 0.1 us)
Async XLA Ops:
  0.0 63.4 %copy-start = (bf16[4096,128]{1,0:T(8,128)(2,1)S(1)}, bf16[4096,128]{1,0:T(8,128)(2,1)}, u32[]{:S(2)}) copy-start(bf16[4096,128]{1,0:T(8,128)(2,1)} %param.24) | copy-start | bytes 3145732
  2.5 1.0 copy-start.2
  68.3 4.0 %copy-start.1 = (bf16[320,128,128]{2,1,0:T(8,128)(2,1)S(1)}, bf16[320,128,128]{2,1,0:T(8,128)(2,1)}, u32[]{:S(2)}) copy-start(bf16[320,128,128]{2,1,0:T(8,128)(2,1)} %data.1) | copy-start | bytes 31457284
  72.3 0.7 copy-start.3
  73.0 0.7 copy-start.4

commit v2 on v0

v2 whole, which is shorter than its diff:
```python
import functools

import jax
import jax.numpy as jnp
from jax import lax
from jax.experimental import pallas as pl
from jax.experimental.pallas import tpu as pltpu
from jax.sharding import PartitionSpec as P

MESH = pl.DeviceIdType.MESH
HBM = pl.BlockSpec(memory_space=pltpu.HBM)
VMEM = pl.BlockSpec(memory_space=pltpu.VMEM)
SMEM = pl.BlockSpec(memory_space=pltpu.SMEM)
DMA = pltpu.SemaphoreType.DMA
F32, BF16, I32 = jnp.float32, jnp.bfloat16, jnp.int32


def place(zs):
    wide, n = lax.axis_index("wide"), lax.axis_index("narrow")
    return wide // zs, lax.rem(wide, zs), n


def line_stages(zs):
    order = [0]
    for d in range(1, zs // 2 + 1):
        order += [d] if 2 * d == zs else [d, zs - d]
    if zs < 8:
        return order, [(0, 1), (1, zs)]
    return order, [(0, 1), (1, 3), (3, 5), (5, zs)]


def kernel(
    peers, ns, upo, unroll, parts,
    user_need, item_need, user_slot, item_slot, tile_user, tile_word, tile_month, tile_before, tile_last,
    data, factor, words, months,
    out,
    row_s, table_s, before_s, last_s,
    needs, table, flat, index_v, last_v, held, packed, landed, fetched, words_in, months_in, words_f, months_f,
    scale, buffer, chain, sending, arrived, sums, leaving, final,
    local_sem, held_sem, words_sem, months_sem, data_sem,
    table_send, table_recv, line_send, line_recv, pack_send, pack_recv,
    plane_send, plane_recv, last_send, last_recv,
):
    zs = qs = ns
    x, z, n = place(zs)
    me = x * ns + n
    tiles = buffer.shape[0]
    rows = held[0].shape[1]
    owned_u, owned_i = held[0].shape[0], leaving.shape[1] * leaving.shape[2]
    used, touched = user_need.shape[1], item_need.shape[1]
    each = owned_i // ns
    order, stages = line_stages(zs)

    def plane(p):
        return (p // ns * zs + z, lax.rem(p, ns))

    def sheet(d, m):
        return (x * zs + lax.rem(z + d, zs), lax.rem(n + m, ns))

    def remote(source, target, send, recv, device):
        return pltpu.make_async_remote_copy(
            src_ref=source, dst_ref=target, send_sem=send, recv_sem=recv, device_id=device, device_id_type=MESH
        )

    barrier = pltpu.get_barrier_semaphore()

    @pl.loop(1, peers)
    def _(r):
        pl.semaphore_signal(barrier, inc=1, device_id=plane(lax.rem(me + r, peers)), device_id_type=MESH)

    @pl.loop(ns, zs * ns)
    def _(r):
        pl.semaphore_signal(barrier, inc=1, device_id=sheet(r // ns, lax.rem(r, ns)), device_id_type=MESH)

    words_copy = pltpu.make_async_copy(words, words_in, words_sem)
    months_copy = pltpu.make_async_copy(months, months_in, months_sem)
    words_copy.start()
    months_copy.start()
    held_copy = pltpu.make_async_copy(factor.at[:, lax.rem(ns - n, qs)], held[0], held_sem)
    held_copy.start()

    for k in range(row_s.shape[1] - used - touched):
        row_s[0, used + touched + k] = 0

    @pl.loop(0, used)
    def _(k):
        row_s[0, k] = lax.rem(user_slot[user_need[0, k]], owned_u)

    @pl.loop(0, touched)
    def _(k):
        row_s[0, used + k] = lax.rem(item_slot[item_need[0, k]], owned_i)

    row_copy = pltpu.make_async_copy(row_s, needs, local_sem)
    row_copy.start()
    row_copy.wait()

    pl.semaphore_wait(barrier, peers - 1 + (zs - 1) * ns)

    def table_copy(p, slot, r):
        return remote(needs, table.at[slot], table_send.at[r], table_recv.at[slot], plane(p))

    def line_copy(d, chunk):
        return remote(factor.at[:, chunk], held[d], line_send.at[d], line_recv.at[d], sheet(zs - d, 0))

    def pack_copy(stage, p, slot, r):
        a, b = stages[stage]
        span = pl.ds(a * upo, (b - a) * upo)
        return remote(
            packed.at[r, span], landed.at[slot, span],
            pack_send.at[stage, r], pack_recv.at[stage, slot], plane(p),
        )

    @pl.loop(1, peers)
    def _(r):
        table_copy(lax.rem(me + r, peers), me, r).start()

    for d in order[1:]:
        line_copy(d, lax.rem(d + ns - n, qs)).start()

    per = tiles // parts

    def data_copy(c):
        span = pl.ds(c * per, per)
        return pltpu.make_async_copy(data.at[span], buffer.at[span], data_sem.at[c])

    @pl.loop(0, parts)
    def _(c):
        data_copy(c).start()

    table[me] = needs[...]

    words_copy.wait()
    months_copy.wait()
    words_f[...] = words_in[...].astype(F32)
    months_f[...] = months_in[...].astype(F32)

    @pl.loop(0, tiles // 8)
    def _(s):
        for k in range(8):
            t = s * 8 + k
            scale[pl.ds(t, 1), :] = words_f[pl.ds(tile_word[t], 1), :] * months_f[pl.ds(tile_month[t], 1), :]

    @pl.loop(1, peers)
    def _(r):
        p = lax.rem(me + r, peers)
        table_copy(p, p, r).wait_recv()

    to_scalar = pltpu.make_async_copy(table, table_s, local_sem)
    to_scalar.start()
    to_scalar.wait()

    def pack(stage, p, target, at):
        for pos in range(*stages[stage]):
            d = order[pos]
            owner = x * zs + lax.rem(z + d, zs)
            for i in range(upo):
                target[at, pos * upo + i] = held[d][table_s[p, 0, owner * upo + i]]

    for stage, (a, b) in enumerate(stages):
        if stage == 0:
            held_copy.wait()
        for pos in range(max(a, 1), b):
            line_copy(order[pos], 0).wait_recv()

        @pl.loop(1, peers)
        def _(r):
            p = lax.rem(me + r, peers)
            pack(stage, p, packed, r)
            pack_copy(stage, p, me, r).start()

        pack(stage, me, landed, me)

    @pl.loop(0, peers)
    def _(p):
        flat[pl.ds(p, 1), :] = table[p]

    lanes = flat.shape[1]
    lane = lax.broadcasted_iota(I32, (peers, lanes), 1)
    sub = lax.broadcasted_iota(I32, (peers, lanes), 0)
    slots_lane = lax.broadcasted_iota(I32, (owned_i, lanes), 1)
    slots_sub = lax.broadcasted_iota(I32, (owned_i, lanes), 0)
    entries = flat[...]
    befores, lasts = jnp.zeros((peers, lanes), I32), jnp.zeros((owned_i, lanes), I32)
    for q in range(qs):
        column = used + x * zs + lax.rem(z + lax.rem(n + q, zs), zs)
        down = jnp.sum(jnp.where(lane == column, entries, 0), axis=1, keepdims=True)
        down = jnp.broadcast_to(down, (peers, lanes))
        along = jnp.sum(jnp.where(lane == sub, down, 0), axis=0, keepdims=True)
        same = (down == jnp.broadcast_to(along, (peers, lanes))) & (lane < sub)
        before = jnp.max(jnp.where(same, lane + 1, 0), axis=1, keepdims=True)
        befores = jnp.where(lane == q, jnp.broadcast_to(before, (peers, lanes)), befores)
        mine = (jnp.broadcast_to(along, (owned_i, lanes)) == slots_sub) & (slots_lane < peers)
        last = jnp.max(jnp.where(mine, slots_lane + 1, 0), axis=1, keepdims=True)
        lasts = jnp.where(slots_lane == q, jnp.broadcast_to(last, (owned_i, lanes)), lasts)
    index_v[...] = befores
    last_v[...] = lasts
    index_copy = pltpu.make_async_copy(index_v, before_s, local_sem)
    index_copy.start()
    index_copy.wait()
    final_copy = pltpu.make_async_copy(last_v, last_s, local_sem)
    final_copy.start()
    final_copy.wait()

    chain[0] = jnp.zeros_like(chain[0])
    sums[0] = jnp.zeros_like(sums[0])

    def unpack(stage, p):
        px, pn = p // ns, lax.rem(p, ns)
        for pos in range(*stages[stage]):
            d = order[pos]
            owner = px * zs + lax.rem(z + d, zs)
            q = lax.rem(d + ns - pn, qs)
            at = pl.ds(pl.multiple_of(q * rows, rows), rows)
            for i in range(upo):
                fetched[owner * upo + i, at, :] = landed[p, pos * upo + i]

    for stage in range(len(stages)):
        unpack(stage, me)

        @pl.loop(1, peers)
        def _(r):
            p = lax.rem(me + peers - r, peers)
            pack_copy(stage, p, p, r).wait_recv()
            unpack(stage, p)

    @pl.loop(0, parts)
    def _(c):
        data_copy(c).wait()

    @pl.loop(0, tiles // unroll)
    def _(s):
        terms = []
        for k in range(unroll):
            t = s * unroll + k
            scaled = (fetched[tile_user[t]].astype(F32) * scale[pl.ds(t, 1), :]).astype(BF16)
            terms.append(
                lax.dot_general(buffer[t], scaled, (((0,), (0,)), ((), ())), preferred_element_type=F32)
            )
        for k, term in enumerate(terms):
            t = s * unroll + k
            chain[t + 1] = chain[tile_before[t]] + term

    steps = plane_send.shape[0]
    group = qs // steps

    def plane_copy(step, p, slot, r):
        return remote(
            sending.at[step, p], arrived.at[step, slot], plane_send.at[step, r], plane_recv.at[step, slot], plane(p)
        )

    def load(step, p, target, at):
        px, pn = p // ns, lax.rem(p, ns)
        for j in range(group):
            q = step * group + j
            k = px * zs + lax.rem(z + lax.rem(pn + q, zs), zs)
            target[step, at, j] = chain[tile_last[k], q * rows : (q + 1) * rows, :].astype(BF16)

    for step in range(steps):
        @pl.loop(1, peers)
        def _(r):
            p = lax.rem(me + r, peers)
            load(step, p, sending, p)
            plane_copy(step, p, me, r).start()

        load(step, me, arrived, me)

    def last_copy(q, d, m, source):
        return remote(
            leaving.at[q, lax.rem(n + m, ns)], final.at[source, q],
            last_send.at[q * ns + m], last_recv.at[source * qs + q], sheet(d, m),
        )

    for step in range(steps):
        @pl.loop(1, peers)
        def _(r):
            p = lax.rem(me + peers - r, peers)
            plane_copy(step, p, p, r).wait_recv()

        @pl.loop(0, peers)
        def _(i):
            for j in range(group):
                q = step * group + j
                sums[i + 1, q] = sums[before_s[i, q], q] + arrived[step, i, j].astype(F32)

        for j in range(group):
            q = step * group + j
            d = lax.rem(n + q, zs)
            for slot in range(owned_i):
                leaving[q, slot // each, slot % each] = sums[last_s[slot, q], q].astype(BF16)

            @pl.when(d == 0)
            def _():
                final[z, q] = leaving[q, n]

                @pl.loop(1, ns)
                def _(m):
                    last_copy(q, d, m, z).start()

            @pl.when(d != 0)
            def _():
                @pl.loop(0, ns)
                def _(m):
                    last_copy(q, d, m, z).start()

    for q in range(qs):
        @pl.when(lax.rem(n + q, zs) != 0)
        def _():
            last_copy(q, 1, 0, z).wait_recv()

        @pl.loop(1, zs)
        def _(d):
            last_copy(q, 1, 0, lax.rem(z + d, zs)).wait_recv()

        for s in range(each):
            value = final[0, q, s].astype(F32)
            for source in range(1, zs):
                value += final[source, q, s].astype(F32)
            out[s, q] = value

    @pl.loop(1, peers)
    def _(r):
        table_copy(me, me, r).wait_send()
        for stage in range(len(stages)):
            pack_copy(stage, me, me, r).wait_send()
        for step in range(steps):
            plane_copy(step, me, me, r).wait_send()

    for d in order[1:]:
        line_copy(d, 0).wait_send()

    for q in range(qs):
        @pl.when(lax.rem(n + q, zs) != 0)
        def _():
            last_copy(q, 1, 0, z).wait_send()

        @pl.loop(1, ns)
        def _(m):
            last_copy(q, 1, m, z).wait_send()


def shards(
    tile_data,
    tile_user,
    tile_item,
    tile_word,
    tile_month,
    tile_live,
    user_need,
    item_need,
    user_slot,
    item_slot,
    user_factor,
    word_factor,
    month_factor,
):
    wide, ns = lax.axis_size("wide"), lax.axis_size("narrow")
    zs = qs = ns
    peers = wide // zs * ns
    tiles, side = tile_data.shape[:2]
    rank = user_factor.shape[1]
    rows = side // qs
    owned_u, owned_i = user_slot.shape[0] // wide, item_slot.shape[0] // wide
    used, touched = user_need.shape[1], item_need.shape[1]
    upo, each = used // wide, owned_i // ns
    lanes = -(-(used + touched) // 128) * 128
    stages = len(line_stages(zs)[1])
    steps = min(4, qs)
    parts = min(16, tiles // 16)

    index = lax.iota(I32, tiles)
    same = (tile_item[:, None] == tile_item[None, :]) & (index[None, :] < index[:, None])
    tile_before = jnp.max(jnp.where(same, index[None, :] + 1, 0), axis=1)
    mine = (tile_item[None, :] == lax.iota(I32, touched)[:, None]) & (index < tile_live[0])[None, :]
    tile_last = jnp.max(jnp.where(mine, index[None, :] + 1, 0), axis=1)

    out = pl.pallas_call(
        functools.partial(kernel, peers, ns, upo, 16, parts),
        out_shape=jax.ShapeDtypeStruct((each, qs, rows, rank), F32),
        in_specs=[SMEM] * 9 + [HBM] * 4,
        out_specs=VMEM,
        scratch_shapes=[
            pltpu.SMEM((1, lanes), I32),
            pltpu.SMEM((peers, 1, lanes), I32),
            pltpu.SMEM((peers, lanes), I32),
            pltpu.SMEM((owned_i, lanes), I32),
            pltpu.VMEM((1, lanes), I32),
            pltpu.VMEM((peers, 1, lanes), I32),
            pltpu.VMEM((peers, lanes), I32),
            pltpu.VMEM((peers, lanes), I32),
            pltpu.VMEM((owned_i, lanes), I32),
            [pltpu.VMEM((owned_u, rows, rank), BF16)] * zs,
            pltpu.VMEM((peers, zs * upo, rows, rank), BF16),
            pltpu.VMEM((peers, zs * upo, rows, rank), BF16),
            pltpu.VMEM((used, side, rank), BF16),
            pltpu.VMEM(word_factor.shape, BF16),
            pltpu.VMEM(month_factor.shape, BF16),
            pltpu.VMEM(word_factor.shape, F32),
            pltpu.VMEM(month_factor.shape, F32),
            pltpu.VMEM((tiles, rank), F32),
            pltpu.VMEM((tiles, side, side), BF16),
            pltpu.VMEM((tiles + 1, side, rank), F32),
            pltpu.VMEM((steps, peers, qs // steps, rows, rank), BF16),
            pltpu.VMEM((steps, peers, qs // steps, rows, rank), BF16),
            pltpu.VMEM((peers + 1, qs, rows, rank), F32),
            pltpu.VMEM((qs, ns, each, rows, rank), BF16),
            pltpu.VMEM((zs, qs, each, rows, rank), BF16),
            DMA,
            DMA,
            DMA,
            DMA,
            DMA((parts,)),
            DMA((peers,)),
            DMA((peers,)),
            DMA((zs,)),
            DMA((zs,)),
            DMA((stages, peers)),
            DMA((stages, peers)),
            DMA((steps, peers)),
            DMA((steps, peers)),
            DMA((qs * ns,)),
            DMA((zs * qs,)),
        ],
        compiler_params=pltpu.CompilerParams(
            collective_id=0, has_side_effects=True, vmem_limit_bytes=58 << 20
        ),
        name="mttkrp",
    )(
        user_need, item_need, user_slot, item_slot, tile_user, tile_word, tile_month, tile_before, tile_last,
        tile_data, user_factor.reshape(owned_u, qs, rows, rank), word_factor, month_factor,
    )
    return out.reshape(-1, rank)


def solution(mesh):
    return jax.shard_map(
        shards,
        mesh=mesh,
        in_specs=(
            P(("wide", "narrow"), None, None),
            P(("wide", "narrow")),
            P(("wide", "narrow")),
            P(("wide", "narrow")),
            P(("wide", "narrow")),
            P(("wide", "narrow")),
            P(("wide", "narrow"), None),
            P(("wide", "narrow"), None),
            P(),
            P(),
            P("wide", None),
            P(),
            P(),
        ),
        out_specs=P(("wide", "narrow"), None),
        check_vma=False,
    )
```

time: 348 us -> 95.3 us (0.27)
  waiting for transfers between devices: 203 us -> 0 us
  Pallas kernels: 0 us -> 90 us
  local copies, waits for them, and re-layouts: 48.7 us -> 1.57 us
  other arithmetic: 46.7 us -> 2.89 us
  starting transfers between devices: 17.2 us -> 0 us
  matrix products: 14.9 us -> 0 us
  between operations: 14.1 us -> 0.67 us
    all_gather x1 -> x0, waiting for transfers between devices: 123 us -> none  [shards(): gathered = lax.all_gather(user_factor, 'wide', axis=0, tiled=True)]
    pallas_call x0 -> x1, Pallas kernels: none -> 90 us  [shards(): pl.pallas_call(functools.partial(kernel, peers, ns, upo, 16, parts), out_...]
    all_to_all x2 -> x0, waiting for transfers between devices: 48 us -> none  [the longest x1 48 us: shards(): lax.all_to_all(partial_value.reshape(wide_count, -1, block_side, rank_wid...]
    scatter-add x1 -> x0, other arithmetic: 41.9 us -> none  [shards(): jax.ops.segment_sum(contrib, group_ids, num_segments=touched + 1)[:touched]]
    reduce_scatter x1 -> x0, waiting for transfers between devices: 31.5 us -> none  [shards(): lax.psum_scatter(owner_sum, 'narrow', scatter_dimension=0, tiled=True)]
    gather x6 -> x0, local copies, waits for them, and re-layouts: 23.9 us -> none  [the longest x1 10.7 us: shards(): fetched[tile_user].astype(jnp.float32) * word_month[:, None, :]]
    dot_general x2 -> x0, local copies, waits for them, and re-layouts: 22.4 us -> none  [the longest x1 21.1 us: shards(): jnp.einsum('tab,tar->tbr', tile_data, scaled, preferred_element_type=jnp....]
    all_to_all x2 -> x0, starting transfers between devices: 17.1 us -> none  [the longest x1 11.9 us: shards(): lax.all_to_all(item_local, 'wide', split_axis=0, concat_axis=0, tiled=True)]
  transfers between devices with their start and end apart: 4 -> 0, of which waited for: 3 -> 0; matrix products, arithmetic and copies ran while one was open for 31% -> 0% of each run, Pallas kernels for 0% -> 0%
where the time goes in v2:
time: 95.3 us; the launch traced here: 95.1 us
  Pallas kernels  90 us (94%)
  other arithmetic  2.89 us (3%)
  local copies, waits for them, and re-layouts  1.57 us (2%)
    pallas_call x1, Pallas kernels, shards(): pl.pallas_call(functools.partial(kernel, peers, ns, upo, 16, parts), out_...  90 us

profile of v2, /device:TPU:1, one launch (start us, length us, event | category | flops | bytes accessed | tf_op | source)
XLA Modules:
  0.0 95.1 jit_solution(5428098788716092558)
XLA Ops:
  0.7 1.3 %select_reduce_fusion.1.tile_last = s32[32]{0:T(128)} fusion(s32[320]{0:T(512)S(1)} %iota_add_fusion, s32[320]{0:T(512)} %param.15, pred[320]{0:T(512)(128)(4,1)S(1)} %iota_compare_fusion.2), kind=kLoop, calls=%fused_computation.3 | loop fusion | flops 40928 | bytes 3008 | tf_op jit(solution)/shard_map/reduce_max | solution.py:374
  2.0 1.6 %select_reduce_fusion.tile_before = s32[320]{0:T(512)} fusion(s32[320]{0:T(512)S(1)} %iota_add_fusion, s32[320]{0:T(512)} %param.15), kind=kLoop, calls=%fused_computation | loop fusion | flops 511680 | bytes 3840 | tf_op jit(solution)/shard_map/reduce_max | solution.py:372
  3.6 90.0 %mttkrp.1 = f32[2,8,16,128]{3,2,1,0:T(8,128)} custom-call(s32[1,64]{1,0:T(1,128)} %user_need.1, s32[1,32]{1,0:T(1,128)} %item_need.1, s32[512]{0:T(512)} %user_slot.1, s32[512]{0:T(512)} %item_slot.1, s32[320]{0:T(512)} %tile_user.1, s32[320]{0:T(512)} %tile_word.1, s32[320]{0:T(512)} %tile_month.1, s32[320]{0:T(512)} %select_reduce_fusion.tile_before, ...), custom_call_target="tpu_custom_call" | custom-call | tf_op jit(solution)/shard_map/mttkrp/pallas_call | solution.py:376
  93.5 1.6 %copy.16 = f32[256,128]{1,0:T(8,128)} copy(f32[256,128]{1,0:T(8,128)} %bitcast.5) | data formatting | bytes 262144
  (2 shorter events, 0.0 us)

commit v3 on v2

--- a/solution.py
+++ b/solution.py
@@ -9,8 +9,6 @@
 
 MESH = pl.DeviceIdType.MESH
 HBM = pl.BlockSpec(memory_space=pltpu.HBM)
-VMEM = pl.BlockSpec(memory_space=pltpu.VMEM)
-SMEM = pl.BlockSpec(memory_space=pltpu.SMEM)
 DMA = pltpu.SemaphoreType.DMA
 F32, BF16, I32 = jnp.float32, jnp.bfloat16, jnp.int32
 
@@ -30,14 +28,15 @@
 
 
 def kernel(
-    peers, ns, upo, unroll, parts,
-    user_need, item_need, user_slot, item_slot, tile_user, tile_word, tile_month, tile_before, tile_last,
-    data, factor, words, months,
-    out,
-    row_s, table_s, before_s, last_s,
-    needs, table, flat, index_v, last_v, held, packed, landed, fetched, words_in, months_in, words_f, months_f,
-    scale, buffer, chain, sending, arrived, sums, leaving, final,
-    local_sem, held_sem, words_sem, months_sem, data_sem,
+    peers, ns, upo, unroll,
+    user_need_h, item_need_h, user_slot_h, item_slot_h, tile_user_h, tile_word_h, tile_month_h, tile_live_h,
+    tile_item_h, data, factor, words, months,
+    final,
+    user_need, item_need, user_slot, item_slot, tile_user, tile_word, tile_month, tile_live,
+    row_s, table_s, before_s, last_s, tile_before, tile_last,
+    items_v, tile_before_v, tile_last_v, needs, table, flat, index_v, last_v, held, packed, landed, fetched, words_in, months_in, words_f, months_f,
+    scale, buffer, chain, sending, arrived, sums, leaving,
+    small_sem, items_sem, stay_sem, local_sem, held_sem, words_sem, months_sem, data_sem,
     table_send, table_recv, line_send, line_recv, pack_send, pack_recv,
     plane_send, plane_recv, last_send, last_recv,
 ):
@@ -72,6 +71,17 @@
     def _(r):
         pl.semaphore_signal(barrier, inc=1, device_id=sheet(r // ns, lax.rem(r, ns)), device_id_type=MESH)
 
+    small = [
+        pltpu.make_async_copy(source, target, small_sem.at[i])
+        for i, (source, target) in enumerate((
+            (user_need_h, user_need), (item_need_h, item_need), (user_slot_h, user_slot), (item_slot_h, item_slot),
+            (tile_user_h, tile_user), (tile_word_h, tile_word), (tile_month_h, tile_month), (tile_live_h, tile_live),
+        ))
+    ]
+    for copy in small:
+        copy.start()
+    items_copy = pltpu.make_async_copy(tile_item_h, items_v, items_sem)
+    items_copy.start()
     words_copy = pltpu.make_async_copy(words, words_in, words_sem)
     months_copy = pltpu.make_async_copy(months, months_in, months_sem)
     words_copy.start()
@@ -79,6 +89,9 @@
     held_copy = pltpu.make_async_copy(factor.at[:, lax.rem(ns - n, qs)], held[0], held_sem)
     held_copy.start()
 
+    for copy in small:
+        copy.wait()
+
     for k in range(row_s.shape[1] - used - touched):
         row_s[0, used + touched + k] = 0
 
@@ -97,17 +110,17 @@
     pl.semaphore_wait(barrier, peers - 1 + (zs - 1) * ns)
 
     def table_copy(p, slot, r):
-        return remote(needs, table.at[slot], table_send.at[r], table_recv.at[slot], plane(p))
+        return remote(needs, table.at[slot], table_send, table_recv, plane(p))
 
     def line_copy(d, chunk):
-        return remote(factor.at[:, chunk], held[d], line_send.at[d], line_recv.at[d], sheet(zs - d, 0))
+        return remote(factor.at[:, chunk], held[d], line_send, line_recv.at[d], sheet(zs - d, 0))
 
     def pack_copy(stage, p, slot, r):
         a, b = stages[stage]
         span = pl.ds(a * upo, (b - a) * upo)
         return remote(
             packed.at[r, span], landed.at[slot, span],
-            pack_send.at[stage, r], pack_recv.at[stage, slot], plane(p),
+            pack_send.at[stage], pack_recv.at[stage], plane(p),
         )
 
     @pl.loop(1, peers)
@@ -117,16 +130,8 @@
     for d in order[1:]:
         line_copy(d, lax.rem(d + ns - n, qs)).start()
 
-    per = tiles // parts
-
-    def data_copy(c):
-        span = pl.ds(c * per, per)
-        return pltpu.make_async_copy(data.at[span], buffer.at[span], data_sem.at[c])
-
-    @pl.loop(0, parts)
-    def _(c):
-        data_copy(c).start()
-
+    data_copy = pltpu.make_async_copy(data, buffer, data_sem)
+    data_copy.start()
     table[me] = needs[...]
 
     words_copy.wait()
@@ -140,10 +145,42 @@
             t = s * 8 + k
             scale[pl.ds(t, 1), :] = words_f[pl.ds(tile_word[t], 1), :] * months_f[pl.ds(tile_month[t], 1), :]
 
-    @pl.loop(1, peers)
-    def _(r):
-        p = lax.rem(me + r, peers)
-        table_copy(p, p, r).wait_recv()
+    items_copy.wait()
+    wide = 128
+    pieces = -(-tiles // wide)
+    lane = lax.broadcasted_iota(I32, (wide, wide), 1)
+    sub = lax.broadcasted_iota(I32, (wide, wide), 0)
+    down, along = [], []
+    for c in range(pieces):
+        size = min(wide, tiles - c * wide)
+        line = jnp.broadcast_to(items_v[c * wide : c * wide + size].reshape(1, size), (wide, size))
+        if size < wide:
+            line = jnp.concatenate([line, jnp.full((wide, wide - size), -1, I32)], axis=1)
+        column = jnp.sum(jnp.where(lane == sub, line, 0), axis=1, keepdims=True)
+        along.append(line)
+        down.append(jnp.broadcast_to(column, (wide, wide)))
+    latest = jnp.zeros((1, wide), I32)
+    for c in range(pieces):
+        number = sub + (c * wide + 1)
+        mine = (down[c] == lane) & (number <= tile_live[0])
+        latest = jnp.maximum(latest, jnp.max(jnp.where(mine, number, 0), axis=0, keepdims=True))
+        before = jnp.zeros((1, wide), I32)
+        for b in range(c + 1):
+            number = sub + (b * wide + 1)
+            same = (down[b] == along[c]) & (number < lane + (c * wide + 1))
+            before = jnp.maximum(before, jnp.max(jnp.where(same, number, 0), axis=0, keepdims=True))
+        tile_before_v[:, c * wide : (c + 1) * wide] = before
+    tile_last_v[...] = latest
+    before_copy = pltpu.make_async_copy(tile_before_v, tile_before, local_sem)
+    before_copy.start()
+    before_copy.wait()
+    latest_copy = pltpu.make_async_copy(tile_last_v, tile_last, local_sem)
+    latest_copy.start()
+    latest_copy.wait()
+
+    others = pl.ds(0, peers - 1)
+    table_all = remote(table.at[others], table.at[others], table_send, table_recv, plane(me))
+    table_all.wait_recv()
 
     to_scalar = pltpu.make_async_copy(table, table_s, local_sem)
     to_scalar.start()
@@ -214,18 +251,21 @@
             for i in range(upo):
                 fetched[owner * upo + i, at, :] = landed[p, pos * upo + i]
 
+    def pack_all(stage):
+        a, b = stages[stage]
+        span = pl.ds(a * upo, (b - a) * upo)
+        return remote(
+            packed.at[others, span], landed.at[others, span], pack_send.at[stage], pack_recv.at[stage], plane(me)
+        )
+
     for stage in range(len(stages)):
-        unpack(stage, me)
-
-        @pl.loop(1, peers)
-        def _(r):
-            p = lax.rem(me + peers - r, peers)
-            pack_copy(stage, p, p, r).wait_recv()
+        pack_all(stage).wait_recv()
+
+        @pl.loop(0, peers)
+        def _(p):
             unpack(stage, p)
 
-    @pl.loop(0, parts)
-    def _(c):
-        data_copy(c).wait()
+    data_copy.wait()
 
     @pl.loop(0, tiles // unroll)
     def _(s):
@@ -238,14 +278,14 @@
             )
         for k, term in enumerate(terms):
             t = s * unroll + k
-            chain[t + 1] = chain[tile_before[t]] + term
+            chain[t + 1] = chain[tile_before[0, t]] + term
 
     steps = plane_send.shape[0]
     group = qs // steps
 
     def plane_copy(step, p, slot, r):
         return remote(
-            sending.at[step, p], arrived.at[step, slot], plane_send.at[step, r], plane_recv.at[step, slot], plane(p)
+            sending.at[step, p], arrived.at[step, slot], plane_send.at[step], plane_recv.at[step], plane(p)
         )
 
     def load(step, p, target, at):
@@ -253,7 +293,7 @@
         for j in range(group):
             q = step * group + j
             k = px * zs + lax.rem(z + lax.rem(pn + q, zs), zs)
-            target[step, at, j] = chain[tile_last[k], q * rows : (q + 1) * rows, :].astype(BF16)
+            target[step, at, j] = chain[tile_last[0, k], q * rows : (q + 1) * rows, :].astype(BF16)
 
     for step in range(steps):
         @pl.loop(1, peers)
@@ -264,17 +304,21 @@
 
         load(step, me, arrived, me)
 
-    def last_copy(q, d, m, source):
+    def last_copy(far, q, d, m):
         return remote(
-            leaving.at[q, lax.rem(n + m, ns)], final.at[source, q],
-            last_send.at[q * ns + m], last_recv.at[source * qs + q], sheet(d, m),
-        )
+            leaving.at[q, lax.rem(n + m, ns)], final.at[z, :, q], last_send.at[far], last_recv.at[far], sheet(d, m)
+        )
+
+    def plane_all(step):
+        return remote(
+            sending.at[step, others], arrived.at[step, others], plane_send.at[step], plane_recv.at[step], plane(me)
+        )
+
+    def stay_copy(q):
+        return pltpu.make_async_copy(leaving.at[q, n], final.at[z, :, q], stay_sem)
 
     for step in range(steps):
-        @pl.loop(1, peers)
-        def _(r):
-            p = lax.rem(me + peers - r, peers)
-            plane_copy(step, p, p, r).wait_recv()
+        plane_all(step).wait_recv()
 
         @pl.loop(0, peers)
         def _(i):
@@ -290,52 +334,34 @@
 
             @pl.when(d == 0)
             def _():
-                final[z, q] = leaving[q, n]
+                stay_copy(q).start()
 
                 @pl.loop(1, ns)
                 def _(m):
-                    last_copy(q, d, m, z).start()
+                    last_copy(0, q, d, m).start()
 
             @pl.when(d != 0)
             def _():
                 @pl.loop(0, ns)
                 def _(m):
-                    last_copy(q, d, m, z).start()
-
-    for q in range(qs):
-        @pl.when(lax.rem(n + q, zs) != 0)
-        def _():
-            last_copy(q, 1, 0, z).wait_recv()
-
-        @pl.loop(1, zs)
-        def _(d):
-            last_copy(q, 1, 0, lax.rem(z + d, zs)).wait_recv()
-
-        for s in range(each):
-            value = final[0, q, s].astype(F32)
-            for source in range(1, zs):
-                value += final[source, q, s].astype(F32)
-            out[s, q] = value
-
-    @pl.loop(1, peers)
-    def _(r):
-        table_copy(me, me, r).wait_send()
-        for stage in range(len(stages)):
-            pack_copy(stage, me, me, r).wait_send()
-        for step in range(steps):
-            plane_copy(step, me, me, r).wait_send()
-
-    for d in order[1:]:
-        line_copy(d, 0).wait_send()
-
-    for q in range(qs):
-        @pl.when(lax.rem(n + q, zs) != 0)
-        def _():
-            last_copy(q, 1, 0, z).wait_send()
-
-        @pl.loop(1, ns)
-        def _(m):
-            last_copy(q, 1, m, z).wait_send()
+                    last_copy(1, q, d, m).start()
+
+    most = pl.ds(0, zs - 1)
+    near_all = remote(leaving.at[0, most], final.at[z, :, most], last_send.at[0], last_recv.at[0], sheet(0, 0))
+    far_all = remote(leaving.at[most], final.at[most], last_send.at[1], last_recv.at[1], sheet(0, 0))
+    near_all.wait_recv()
+    far_all.wait_recv()
+    stay_copy(0).wait()
+
+    table_all.wait_send()
+    lines = remote(factor.at[:, most], factor.at[:, most], line_send, line_recv.at[0], sheet(0, 0))
+    lines.wait_send()
+    for stage in range(len(stages)):
+        pack_all(stage).wait_send()
+    for step in range(steps):
+        plane_all(step).wait_send()
+    near_all.wait_send()
+    far_all.wait_send()
 
 
 def shards(
@@ -365,24 +391,30 @@
     lanes = -(-(used + touched) // 128) * 128
     stages = len(line_stages(zs)[1])
     steps = min(4, qs)
-    parts = min(16, tiles // 16)
-
-    index = lax.iota(I32, tiles)
-    same = (tile_item[:, None] == tile_item[None, :]) & (index[None, :] < index[:, None])
-    tile_before = jnp.max(jnp.where(same, index[None, :] + 1, 0), axis=1)
-    mine = (tile_item[None, :] == lax.iota(I32, touched)[:, None]) & (index < tile_live[0])[None, :]
-    tile_last = jnp.max(jnp.where(mine, index[None, :] + 1, 0), axis=1)
-
-    out = pl.pallas_call(
-        functools.partial(kernel, peers, ns, upo, 16, parts),
-        out_shape=jax.ShapeDtypeStruct((each, qs, rows, rank), F32),
-        in_specs=[SMEM] * 9 + [HBM] * 4,
-        out_specs=VMEM,
+
+    final = pl.pallas_call(
+        functools.partial(kernel, peers, ns, upo, 16),
+        out_shape=jax.ShapeDtypeStruct((zs, each, qs, rows, rank), BF16),
+        in_specs=[HBM] * 13,
+        out_specs=HBM,
         scratch_shapes=[
+            pltpu.SMEM(user_need.shape, I32),
+            pltpu.SMEM(item_need.shape, I32),
+            pltpu.SMEM(user_slot.shape, I32),
+            pltpu.SMEM(item_slot.shape, I32),
+            pltpu.SMEM((tiles,), I32),
+            pltpu.SMEM((tiles,), I32),
+            pltpu.SMEM((tiles,), I32),
+            pltpu.SMEM((1,), I32),
             pltpu.SMEM((1, lanes), I32),
             pltpu.SMEM((peers, 1, lanes), I32),
             pltpu.SMEM((peers, lanes), I32),
             pltpu.SMEM((owned_i, lanes), I32),
+            pltpu.SMEM((1, -(-tiles // 128) * 128), I32),
+            pltpu.SMEM((1, 128), I32),
+            pltpu.VMEM((tiles,), I32),
+            pltpu.VMEM((1, -(-tiles // 128) * 128), I32),
+            pltpu.VMEM((1, 128), I32),
             pltpu.VMEM((1, lanes), I32),
             pltpu.VMEM((peers, 1, lanes), I32),
             pltpu.VMEM((peers, lanes), I32),
@@ -403,32 +435,34 @@
             pltpu.VMEM((steps, peers, qs // steps, rows, rank), BF16),
             pltpu.VMEM((peers + 1, qs, rows, rank), F32),
             pltpu.VMEM((qs, ns, each, rows, rank), BF16),
-            pltpu.VMEM((zs, qs, each, rows, rank), BF16),
-            DMA,
-            DMA,
-            DMA,
-            DMA,
-            DMA((parts,)),
-            DMA((peers,)),
-            DMA((peers,)),
+            DMA((8,)),
+            DMA,
+            DMA,
+            DMA,
+            DMA,
+            DMA,
+            DMA,
+            DMA,
+            DMA,
+            DMA,
+            DMA,
             DMA((zs,)),
-            DMA((zs,)),
-            DMA((stages, peers)),
-            DMA((stages, peers)),
-            DMA((steps, peers)),
-            DMA((steps, peers)),
-            DMA((qs * ns,)),
-            DMA((zs * qs,)),
+            DMA((stages,)),
+            DMA((stages,)),
+            DMA((steps,)),
+            DMA((steps,)),
+            DMA((2,)),
+            DMA((2,)),
         ],
         compiler_params=pltpu.CompilerParams(
             collective_id=0, has_side_effects=True, vmem_limit_bytes=58 << 20
         ),
         name="mttkrp",
     )(
-        user_need, item_need, user_slot, item_slot, tile_user, tile_word, tile_month, tile_before, tile_last,
-        tile_data, user_factor.reshape(owned_u, qs, rows, rank), word_factor, month_factor,
+        user_need, item_need, user_slot, item_slot, tile_user, tile_word, tile_month, tile_live,
+        tile_item, tile_data, user_factor.reshape(owned_u, qs, rows, rank), word_factor, month_factor,
     )
-    return out.reshape(-1, rank)
+    return jnp.sum(final.astype(F32), axis=0).reshape(-1, rank)
 
 
 def solution(mesh):

time: 95.3 us -> 85.5 us (0.90)
  Pallas kernels: 90 us -> 82.9 us
  local copies, waits for them, and re-layouts: 1.57 us -> 0 us
  other arithmetic: 2.89 us -> 1.78 us
    pallas_call x1, Pallas kernels: 90 us -> 82.9 us  [shards(): pl.pallas_call(functools.partial(kernel, peers, ns, upo, 16), out_shape=j...]
    reduce_max x2 -> x0, other arithmetic: 2.88 us -> none  [the longest x1 1.57 us: shards(): tile_before = jnp.max(jnp.where(same, index[None, :] + 1, 0), axis=1)]
    reduce_sum x0 -> x1, other arithmetic: none -> 1.78 us  [shards(): return jnp.sum(final.astype(F32), axis=0).reshape(-1, rank)]
    unnamed x1 -> x0, local copies, waits for them, and re-layouts: 1.57 us -> none
where the time goes in v3:
time: 85.5 us; the launch traced here: 85.4 us
  Pallas kernels  82.9 us (97%)
  other arithmetic  1.78 us (2%)
    pallas_call x1, Pallas kernels, shards(): pl.pallas_call(functools.partial(kernel, peers, ns, upo, 16), out_shape=j...  82.9 us
    reduce_sum x1, other arithmetic, shards(): return jnp.sum(final.astype(F32), axis=0).reshape(-1, rank)  1.78 us

profile of v3, /device:TPU:1, one launch (start us, length us, event | category | flops | bytes accessed | tf_op | source)
XLA Modules:
  0.0 85.4 jit_solution(9273864328200574300)
XLA Ops:
  0.7 82.9 %mttkrp.1 = bf16[8,2,8,16,128]{4,3,2,1,0:T(8,128)(2,1)} custom-call(s32[1,64]{1,0:T(1,128)} %user_need_h.1, s32[1,32]{1,0:T(1,128)} %item_need_h.1, s32[512]{0:T(512)} %user_slot_h.1, s32[512]{0:T(512)} %item_slot_h.1, s32[320]{0:T(512)} %tile_user_h.1, s32[320]{0:T(512)} %tile_word_h.1, s32[320]{0:T(512)} %tile_month_h.1, s32[1]{0:T(128)S(6)} %copy.14.tile_live_h, ...), custom_call_target="tpu_custom_call" | custom-call | tf_op jit(solution)/shard_map/mttkrp/pallas_call | solution.py:395
  83.6 1.8 %convert_reduce_fusion = f32[2,8,16,128]{3,2,1,0:T(8,128)} fusion(bf16[8,2,8,16,128]{4,3,2,1,0:T(8,128)(2,1)} %mttkrp.1), kind=kLoop, calls=%fused_computation | loop fusion | flops 491520 | bytes 655360 | tf_op jit(solution)/shard_map/reduce_sum | solution.py:465

commit v4 on v3

--- a/solution.py
+++ b/solution.py
@@ -18,13 +18,11 @@
     return wide // zs, lax.rem(wide, zs), n
 
 
-def line_stages(zs):
+def line_order(zs):
     order = [0]
     for d in range(1, zs // 2 + 1):
         order += [d] if 2 * d == zs else [d, zs - d]
-    if zs < 8:
-        return order, [(0, 1), (1, zs)]
-    return order, [(0, 1), (1, 3), (3, 5), (5, zs)]
+    return order
 
 
 def kernel(
@@ -48,7 +46,8 @@
     owned_u, owned_i = held[0].shape[0], leaving.shape[1] * leaving.shape[2]
     used, touched = user_need.shape[1], item_need.shape[1]
     each = owned_i // ns
-    order, stages = line_stages(zs)
+    order = line_order(zs)
+    stages = [(pos, pos + 1) for pos in range(zs)]
 
     def plane(p):
         return (p // ns * zs + z, lax.rem(p, ns))
@@ -150,27 +149,40 @@
     pieces = -(-tiles // wide)
     lane = lax.broadcasted_iota(I32, (wide, wide), 1)
     sub = lax.broadcasted_iota(I32, (wide, wide), 0)
+
+    def count(mask, axis):
+        return jnp.sum(jnp.where(mask, 1, 0), axis=axis, keepdims=True)
+
+    def spread(value):
+        return jnp.broadcast_to(value, (wide, wide))
+
     down, along = [], []
     for c in range(pieces):
         size = min(wide, tiles - c * wide)
         line = jnp.broadcast_to(items_v[c * wide : c * wide + size].reshape(1, size), (wide, size))
         if size < wide:
-            line = jnp.concatenate([line, jnp.full((wide, wide - size), -1, I32)], axis=1)
-        column = jnp.sum(jnp.where(lane == sub, line, 0), axis=1, keepdims=True)
+            line = jnp.concatenate([line, jnp.full((wide, wide - size), touched + 1, I32)], axis=1)
+        alive = lane + c * wide < tile_live[0]
+        line = jnp.where(alive, line, jnp.maximum(line, touched))
         along.append(line)
-        down.append(jnp.broadcast_to(column, (wide, wide)))
-    latest = jnp.zeros((1, wide), I32)
+        down.append(spread(jnp.sum(jnp.where(lane == sub, line, 0), axis=1, keepdims=True)))
+    reach, present = jnp.zeros((1, wide), I32), jnp.zeros((1, wide), I32)
+    codes = [jnp.zeros((1, wide), I32) for _ in range(pieces)]
     for c in range(pieces):
-        number = sub + (c * wide + 1)
-        mine = (down[c] == lane) & (number <= tile_live[0])
-        latest = jnp.maximum(latest, jnp.max(jnp.where(mine, number, 0), axis=0, keepdims=True))
-        before = jnp.zeros((1, wide), I32)
-        for b in range(c + 1):
-            number = sub + (b * wide + 1)
-            same = (down[b] == along[c]) & (number < lane + (c * wide + 1))
-            before = jnp.maximum(before, jnp.max(jnp.where(same, number, 0), axis=0, keepdims=True))
-        tile_before_v[:, c * wide : (c + 1) * wide] = before
-    tile_last_v[...] = latest
+        reach += count(down[c] <= lane, 0)
+        present += count(down[c] == lane, 0)
+        rank, repeats = jnp.zeros((wide, 1), I32), jnp.zeros((wide, 1), I32)
+        for b in range(pieces):
+            earlier = lane + b * wide < sub + c * wide
+            same = (along[b] == down[c]) & earlier
+            rank += count((along[b] < down[c]) | same, 1)
+            repeats += count(same, 1)
+        code = (sub + c * wide) * 2 + spread(jnp.minimum(repeats, 1))
+        for b in range(pieces):
+            codes[b] += jnp.sum(jnp.where(spread(rank) == lane + b * wide, code, 0), axis=0, keepdims=True)
+    for c in range(pieces):
+        tile_before_v[:, c * wide : (c + 1) * wide] = codes[c]
+    tile_last_v[...] = jnp.where(present > 0, reach, 0)
     before_copy = pltpu.make_async_copy(tile_before_v, tile_before, local_sem)
     before_copy.start()
     before_copy.wait()
@@ -223,11 +235,16 @@
         down = jnp.sum(jnp.where(lane == column, entries, 0), axis=1, keepdims=True)
         down = jnp.broadcast_to(down, (peers, lanes))
         along = jnp.sum(jnp.where(lane == sub, down, 0), axis=0, keepdims=True)
-        same = (down == jnp.broadcast_to(along, (peers, lanes))) & (lane < sub)
-        before = jnp.max(jnp.where(same, lane + 1, 0), axis=1, keepdims=True)
+        along = jnp.broadcast_to(along, (peers, lanes))
+        same = (down == along) & (sub < lane)
+        rank = jnp.broadcast_to(count((down < along) | same, 0), (peers, lanes))
+        code = 2 * lane + jnp.broadcast_to(jnp.minimum(count(same, 0), 1), (peers, lanes))
+        before = jnp.sum(jnp.where((rank == sub) & (lane < peers), code, 0), axis=1, keepdims=True)
         befores = jnp.where(lane == q, jnp.broadcast_to(before, (peers, lanes)), befores)
-        mine = (jnp.broadcast_to(along, (owned_i, lanes)) == slots_sub) & (slots_lane < peers)
-        last = jnp.max(jnp.where(mine, slots_lane + 1, 0), axis=1, keepdims=True)
+        inside = slots_lane < peers
+        target = jnp.broadcast_to(along[:1], (owned_i, lanes))
+        reach = count((target <= slots_sub) & inside, 1)
+        last = jnp.where(count((target == slots_sub) & inside, 1) > 0, reach, 0)
         lasts = jnp.where(slots_lane == q, jnp.broadcast_to(last, (owned_i, lanes)), lasts)
     index_v[...] = befores
     last_v[...] = lasts
@@ -267,25 +284,27 @@
 
     data_copy.wait()
 
-    @pl.loop(0, tiles // unroll)
-    def _(s):
+    def step_tiles(s, total):
         terms = []
         for k in range(unroll):
-            t = s * unroll + k
+            code = tile_before[0, s * unroll + k]
+            t = code // 2
             scaled = (fetched[tile_user[t]].astype(F32) * scale[pl.ds(t, 1), :]).astype(BF16)
-            terms.append(
-                lax.dot_general(buffer[t], scaled, (((0,), (0,)), ((), ())), preferred_element_type=F32)
-            )
-        for k, term in enumerate(terms):
-            t = s * unroll + k
-            chain[t + 1] = chain[tile_before[0, t]] + term
+            term = lax.dot_general(buffer[t], scaled, (((0,), (0,)), ((), ())), preferred_element_type=F32)
+            terms.append((lax.rem(code, 2).astype(F32), term))
+        for k, (keep, term) in enumerate(terms):
+            total = total * keep + term
+            chain[s * unroll + k + 1] = total
+        return total
+
+    lax.fori_loop(0, tiles // unroll, step_tiles, jnp.zeros(chain.shape[1:], F32))
 
     steps = plane_send.shape[0]
     group = qs // steps
 
     def plane_copy(step, p, slot, r):
         return remote(
-            sending.at[step, p], arrived.at[step, slot], plane_send.at[step], plane_recv.at[step], plane(p)
+            sending.at[step, p], arrived[step].at[slot], plane_send.at[step], plane_recv.at[step], plane(p)
         )
 
     def load(step, p, target, at):
@@ -293,16 +312,16 @@
         for j in range(group):
             q = step * group + j
             k = px * zs + lax.rem(z + lax.rem(pn + q, zs), zs)
-            target[step, at, j] = chain[tile_last[0, k], q * rows : (q + 1) * rows, :].astype(BF16)
+            target[at, j] = chain[tile_last[0, k], q * rows : (q + 1) * rows, :].astype(BF16)
 
     for step in range(steps):
         @pl.loop(1, peers)
         def _(r):
             p = lax.rem(me + r, peers)
-            load(step, p, sending, p)
+            load(step, p, sending.at[step], p)
             plane_copy(step, p, me, r).start()
 
-        load(step, me, arrived, me)
+        load(step, me, arrived[step], me)
 
     def last_copy(far, q, d, m):
         return remote(
@@ -311,7 +330,7 @@
 
     def plane_all(step):
         return remote(
-            sending.at[step, others], arrived.at[step, others], plane_send.at[step], plane_recv.at[step], plane(me)
+            sending.at[step, others], arrived[step].at[others], plane_send.at[step], plane_recv.at[step], plane(me)
         )
 
     def stay_copy(q):
@@ -320,11 +339,16 @@
     for step in range(steps):
         plane_all(step).wait_recv()
 
-        @pl.loop(0, peers)
-        def _(i):
-            for j in range(group):
-                q = step * group + j
-                sums[i + 1, q] = sums[before_s[i, q], q] + arrived[step, i, j].astype(F32)
+        for j in range(group):
+            q = step * group + j
+
+            def add(i, total):
+                code = before_s[i, q]
+                total = total * lax.rem(code, 2).astype(F32) + arrived[step][code // 2, j].astype(F32)
+                sums[i + 1, q] = total
+                return total
+
+            lax.fori_loop(0, peers, add, jnp.zeros(sums.shape[2:], F32), unroll=4)
 
         for j in range(group):
             q = step * group + j
@@ -389,11 +413,11 @@
     used, touched = user_need.shape[1], item_need.shape[1]
     upo, each = used // wide, owned_i // ns
     lanes = -(-(used + touched) // 128) * 128
-    stages = len(line_stages(zs)[1])
-    steps = min(4, qs)
+    stages = zs
+    steps = qs
 
     final = pl.pallas_call(
-        functools.partial(kernel, peers, ns, upo, 16),
+        functools.partial(kernel, peers, ns, upo, 32),
         out_shape=jax.ShapeDtypeStruct((zs, each, qs, rows, rank), BF16),
         in_specs=[HBM] * 13,
         out_specs=HBM,
@@ -432,7 +456,7 @@
             pltpu.VMEM((tiles, side, side), BF16),
             pltpu.VMEM((tiles + 1, side, rank), F32),
             pltpu.VMEM((steps, peers, qs // steps, rows, rank), BF16),
-            pltpu.VMEM((steps, peers, qs // steps, rows, rank), BF16),
+            [pltpu.VMEM((peers, qs // steps, rows, rank), BF16)] * steps,
             pltpu.VMEM((peers + 1, qs, rows, rank), F32),
             pltpu.VMEM((qs, ns, each, rows, rank), BF16),
             DMA((8,)),

time: 85.5 us -> 81.1 us (0.949)
  Pallas kernels: 82.9 us -> 78.5 us
    pallas_call x1, Pallas kernels: 82.9 us -> 78.5 us  [shards(): pl.pallas_call(functools.partial(kernel, peers, ns, upo, 32), out_shape=j...]
where the time goes in v4:
time: 81.1 us; the launch traced here: 81 us
  Pallas kernels  78.5 us (97%)
  other arithmetic  1.78 us (2%)
    pallas_call x1, Pallas kernels, shards(): pl.pallas_call(functools.partial(kernel, peers, ns, upo, 32), out_shape=j...  78.5 us
    reduce_sum x1, other arithmetic, shards(): return jnp.sum(final.astype(F32), axis=0).reshape(-1, rank)  1.78 us

profile of v4, /device:TPU:1, one launch (start us, length us, event | category | flops | bytes accessed | tf_op | source)
XLA Modules:
  0.0 81.0 jit_solution(3246198970541171351)
XLA Ops:
  0.7 78.5 %mttkrp.1 = bf16[8,2,8,16,128]{4,3,2,1,0:T(8,128)(2,1)} custom-call(s32[1,64]{1,0:T(1,128)} %user_need_h.1, s32[1,32]{1,0:T(1,128)} %item_need_h.1, s32[512]{0:T(512)} %user_slot_h.1, s32[512]{0:T(512)} %item_slot_h.1, s32[320]{0:T(512)} %tile_user_h.1, s32[320]{0:T(512)} %tile_word_h.1, s32[320]{0:T(512)} %tile_month_h.1, s32[1]{0:T(128)S(6)} %copy.14.tile_live_h, ...), custom_call_target="tpu_custom_call" | custom-call | tf_op jit(solution)/shard_map/mttkrp/pallas_call | solution.py:419
  79.2 1.8 %convert_reduce_fusion = f32[2,8,16,128]{3,2,1,0:T(8,128)} fusion(bf16[8,2,8,16,128]{4,3,2,1,0:T(8,128)(2,1)} %mttkrp.1), kind=kLoop, calls=%fused_computation | loop fusion | flops 491520 | bytes 655360 | tf_op jit(solution)/shard_map/reduce_sum | solution.py:489
